TPU v7x, 32 devices: a whole 2x2x4 slice. The times are simulated.
32 devices in a mesh: dp: 8 (over y, x, core), mp: 4 (over z).
Axes of the slice: x: 2, y: 2, z: 4, core: 2. Of those that a mesh axis runs over, the one named last changes fastest.
Arguments:
- hidden_in: bfloat16 [2, 8192, 2048], P(None, ('dp', 'mp')), may hold values from -6 to 6
- counts: int32 [2, 8], P(None, 'dp'), may hold values from 20 to 50, as said below
- summary: float32 [50, 2048], replicated, may hold values from -6 to 6
- query_weight: bfloat16 [2048, 2048], P('dp', 'mp'), may hold values from -0.125 to 0.125
- query_bias: bfloat16 [2048], P('mp'), may hold values from -1.75 to 1.75
- key_weight: bfloat16 [2048, 2048], P('dp', 'mp'), may hold values from -0.125 to 0.125
- value_weight: bfloat16 [2048, 2048], P('dp', 'mp'), may hold values from -0.125 to 0.125
- value_bias: bfloat16 [2048], P('mp'), may hold values from -1.75 to 1.75
- out_weight: bfloat16 [2048, 2048], P('mp', 'dp'), may hold values from -2 to 2
- out_bias: bfloat16 [2048], replicated, may hold values from -1.25 to 1.25
- up_weight: bfloat16 [2048, 8192], P('dp', 'mp'), may hold values from -0.125 to 0.125
- up_bias: bfloat16 [8192], P('mp'), may hold values from -1.75 to 1.75
- down_weight: bfloat16 [8192, 2048], P('mp', 'dp'), may hold values from -0.0625 to 0.0625
- down_bias: bfloat16 [2048], replicated, may hold values from -1.25 to 1.25
- attn_gain: float32 [2048], replicated, may hold values from 0.5 to 1.5
- attn_shift: float32 [2048], replicated, may hold values from -0.625 to 0.625
- mlp_gain: float32 [2048], replicated, may hold values from 0.5 to 1.5
- mlp_shift: float32 [2048], replicated, may hold values from -0.625 to 0.625
- cotangent: bfloat16 [2, 8192, 2048], P(None, ('dp', 'mp')), may hold values from -6 to 6
Outputs:
- layer_out: bfloat16 [2, 8192, 2048], P(None, ('dp', 'mp'))
- grad_input: float32 [2, 8192, 2048], P(None, ('dp', 'mp'))
- grad_summary: float32 [50, 2048], replicated
- grad_query_weight: float32 [2048, 2048], P('dp', 'mp')
- grad_query_bias: float32 [2048], P('mp')
- grad_key_weight: float32 [2048, 2048], P('dp', 'mp')
- grad_value_weight: float32 [2048, 2048], P('dp', 'mp')
- grad_value_bias: float32 [2048], P('mp')
- grad_out_weight: float32 [2048, 2048], P('mp', 'dp')
- grad_out_bias: float32 [2048], replicated
- grad_up_weight: float32 [2048, 8192], P('dp', 'mp')
- grad_up_bias: float32 [8192], P('mp')
- grad_down_weight: float32 [8192, 2048], P('mp', 'dp')
- grad_down_bias: float32 [2048], replicated
- grad_attn_gain: float32 [2048], replicated
- grad_attn_shift: float32 [2048], replicated
- grad_mlp_gain: float32 [2048], replicated
- grad_mlp_shift: float32 [2048], replicated
Inputs may be any that keep to these rules, and one draw needn't show every extreme that they name: `counts`: an item's count c marks the first c of its 50 prefix slots and the first c of its 50 appended slots as used.
All inputs are finite; a program needn't handle non-finite values.
Results may differ from a plain program's by a relative error of at most 0.02.
Values may be sent and summed in bfloat16 or wider, within the bound.
No kernel may reach another device: no remote copies, remote signals or barrier semaphores. Data moves between devices by JAX's collectives and lax.ppermute only.
A program may use at most 256 MiB of HBM per device.

v0:
```python
import math
import jax
import jax.numpy as jnp
from jax import lax
from jax.sharding import PartitionSpec as P

D = 2048
HD = 64
SUMM = 50
precise = lax.Precision.HIGHEST
gelu_coef = math.sqrt(2.0 / math.pi)


def gelu_slope(values_in):
    inner = gelu_coef * (values_in + 0.044715 * values_in * values_in * values_in)
    tangent = jnp.tanh(inner)
    return 0.5 * (1.0 + tangent) + 0.5 * values_in * (1.0 - tangent * tangent) * gelu_coef * (
        1.0 + 3.0 * 0.044715 * values_in * values_in
    )


def layer_norm(values_in, gain_vec, shift_vec):
    centred = values_in - jnp.mean(values_in, axis=-1, keepdims=True)
    spread = jnp.mean(centred * centred, axis=-1, keepdims=True)
    scaled = lax.rsqrt(spread + 1e-05)
    unit_rows = centred * scaled
    return (unit_rows * gain_vec + shift_vec, unit_rows, scaled)


def norm_back(grad_out, unit_rows, scaled, gain_vec):
    weighted = grad_out * gain_vec
    return scaled * (
        weighted
        - jnp.mean(weighted, axis=-1, keepdims=True)
        - unit_rows * jnp.mean(weighted * unit_rows, axis=-1, keepdims=True)
    )


def dense(left_side, right_side):
    return jnp.dot(left_side, right_side, preferred_element_type=jnp.float32)


def times_t(left_side, right_side):
    return lax.dot_general(
        left_side, right_side, (((1,), (1,)), ((), ())), preferred_element_type=jnp.float32
    )


def inner_rows(left_side, right_side):
    return lax.dot_general(
        left_side, right_side, (((0,), (0,)), ((), ())), preferred_element_type=jnp.float32
    )


def live_keys(seq_len, item_count):
    positions = jnp.arange(seq_len, dtype=jnp.int32)
    slot_ids = positions - (seq_len - SUMM)
    return (
        (positions >= SUMM) & (slot_ids < 0)
        | (positions < item_count)
        | (slot_ids >= 0) & (slot_ids < item_count)
    )


def block_mask(row_begin, block_rows, key_live):
    rows_here = row_begin + jnp.arange(block_rows, dtype=jnp.int32)
    columns = jnp.arange(key_live.shape[0], dtype=jnp.int32)
    return (columns[None, :] <= rows_here[:, None]) & key_live[None, :]


def shards(
    hidden_in,
    counts,
    summary,
    query_weight,
    query_bias,
    key_weight,
    value_weight,
    value_bias,
    out_weight,
    out_bias,
    up_weight,
    up_bias,
    down_weight,
    down_bias,
    attn_gain,
    attn_shift,
    mlp_gain,
    mlp_shift,
    cotangent,
):
    micro_total = hidden_in.shape[0]
    local_rows = hidden_in.shape[1]
    seq_len = local_rows * lax.axis_size("mp")
    row_offset = lax.axis_index("mp") * local_rows
    head_cols = query_weight.shape[1]
    ff_cols = up_weight.shape[1]
    local_heads = head_cols // HD
    block_rows = 512
    block_count = seq_len // block_rows
    qk_scale = HD ** (-0.5)
    bias_query = query_bias.astype(jnp.float32)
    bias_value = value_bias.astype(jnp.float32)
    bias_up = up_bias.astype(jnp.float32)
    bias_out = out_bias.astype(jnp.float32)
    bias_down = down_bias.astype(jnp.float32)
    positions = row_offset + jnp.arange(local_rows, dtype=jnp.int32)
    picker = (
        (positions - (seq_len - SUMM))[:, None] == jnp.arange(SUMM, dtype=jnp.int32)[None, :]
    ).astype(jnp.float32)
    summary_rows = jnp.dot(picker, summary, precision=precise)
    full_shapes = (
        (D, head_cols),
        (D, head_cols),
        (D, head_cols),
        (head_cols, D),
        (D, ff_cols),
        (ff_cols, D),
    )
    full_sums = tuple((jnp.zeros(shape_pair, jnp.float32) for shape_pair in full_shapes))
    head_sums = (
        jnp.zeros((head_cols,), jnp.float32),
        jnp.zeros((head_cols,), jnp.float32),
        jnp.zeros((ff_cols,), jnp.float32),
    )
    zero_width = jnp.zeros((D,), jnp.float32)
    row_sums = (
        zero_width,
        zero_width,
        zero_width,
        zero_width,
        zero_width,
        zero_width,
        jnp.zeros((SUMM, D), jnp.float32),
    )
    outputs = []
    input_grads = []
    for micro_step in range(micro_total):
        gathered = (
            lax.all_gather(query_weight, "dp", axis=0, tiled=True),
            lax.all_gather(key_weight, "dp", axis=0, tiled=True),
            lax.all_gather(value_weight, "dp", axis=0, tiled=True),
            lax.all_gather(out_weight, "dp", axis=1, tiled=True),
            lax.all_gather(up_weight, "dp", axis=0, tiled=True),
            lax.all_gather(down_weight, "dp", axis=1, tiled=True),
        )
        query_full, key_full, value_full, out_full, up_full, down_full = gathered
        key_live = live_keys(seq_len, counts[micro_step, 0])
        joined = hidden_in[micro_step].astype(jnp.float32) + summary_rows
        normed, unit_one, scale_one = layer_norm(joined, attn_gain, attn_shift)
        shard_rows = lax.all_gather(normed.astype(jnp.bfloat16), "mp", axis=0, tiled=True)
        query_part = ((dense(shard_rows, query_full) + bias_query) * qk_scale).astype(jnp.bfloat16)
        key_part = dense(shard_rows, key_full).astype(jnp.bfloat16)
        value_part = (dense(shard_rows, value_full) + bias_value).astype(jnp.bfloat16)
        projected = jnp.concatenate((shard_rows, query_part, key_part, value_part), axis=1)
        normed_full = projected[:, :D]
        query_rows = projected[:, D : D + head_cols].reshape(seq_len, local_heads, HD)
        key_rows = projected[:, D + head_cols : D + 2 * head_cols].reshape(seq_len, local_heads, HD)
        value_rows = projected[:, D + 2 * head_cols :].reshape(seq_len, local_heads, HD)

        def forward_block(block_index):
            row_begin = block_index * block_rows
            query_block = lax.dynamic_slice_in_dim(query_rows, row_begin, block_rows, 0)
            scores = jnp.einsum(
                "qhd,khd->hqk", query_block, key_rows, preferred_element_type=jnp.float32
            )
            scores = jnp.where(block_mask(row_begin, block_rows, key_live)[None], scores, -1e30)
            row_top = jnp.max(scores, axis=-1, keepdims=True)
            exp_scores = jnp.exp(scores - row_top)
            exp_total = jnp.sum(exp_scores, axis=-1, keepdims=True)
            weights_low = (exp_scores / exp_total).astype(jnp.bfloat16)
            block_out = jnp.einsum(
                "hqk,khd->qhd", weights_low, value_rows, preferred_element_type=jnp.float32
            )
            return (
                block_out.astype(jnp.bfloat16).reshape(block_rows, head_cols),
                (row_top + jnp.log(exp_total))[..., 0],
            )

        attn_blocks, log_totals = lax.map(forward_block, jnp.arange(block_count, dtype=jnp.int32))
        attended = attn_blocks.reshape(seq_len, head_cols)
        mixed_rows = (
            joined
            + lax.psum_scatter(
                dense(attended, out_full).astype(jnp.bfloat16),
                "mp",
                scatter_dimension=0,
                tiled=True,
            ).astype(jnp.float32)
            + bias_out
        )
        normed_two, unit_two, scale_two = layer_norm(mixed_rows, mlp_gain, mlp_shift)
        expand_shard_rows = lax.all_gather(
            normed_two.astype(jnp.bfloat16), "mp", axis=0, tiled=True
        )
        up_value = dense(expand_shard_rows, up_full) + bias_up
        expanded = jnp.concatenate(
            (expand_shard_rows, jax.nn.gelu(up_value, approximate=True).astype(jnp.bfloat16)),
            axis=1,
        )
        normed_two_full = expanded[:, :D]
        active = expanded[:, D:]
        layer_rows = (
            mixed_rows
            + lax.psum_scatter(
                dense(active, down_full).astype(jnp.bfloat16), "mp", scatter_dimension=0, tiled=True
            ).astype(jnp.float32)
            + bias_down
        )
        outputs.append(layer_rows.astype(jnp.bfloat16))
        grad_rows = cotangent[micro_step]
        grad_layer = grad_rows.astype(jnp.float32)
        mlp_shard_rows = lax.all_gather(grad_rows, "mp", axis=0, tiled=True)
        mlp_up_value = dense(normed_two_full, up_full) + bias_up
        grad_active = times_t(mlp_shard_rows, down_full)
        mlp_grad_up = (grad_active * gelu_slope(mlp_up_value)).astype(jnp.bfloat16)
        spread_grads = jnp.concatenate((mlp_shard_rows, mlp_grad_up), axis=1)
        grad_full = spread_grads[:, :D]
        grad_up = spread_grads[:, D:]
        micro_down = inner_rows(active, grad_full)
        micro_up = inner_rows(normed_two_full, grad_up)
        up_bias_grad = jnp.sum(grad_up.astype(jnp.float32), axis=0)
        grad_normed_two = lax.psum_scatter(
            times_t(grad_up, up_full).astype(jnp.bfloat16), "mp", scatter_dimension=0, tiled=True
        ).astype(jnp.float32)
        grad_mixed = grad_layer + norm_back(grad_normed_two, unit_two, scale_two, mlp_gain)
        attn_shard_rows = lax.all_gather(grad_mixed.astype(jnp.bfloat16), "mp", axis=0, tiled=True)
        spread_attn = jnp.concatenate(
            (attn_shard_rows, times_t(attn_shard_rows, out_full).astype(jnp.bfloat16)), axis=1
        )
        grad_mixed_full = spread_attn[:, :D]
        grad_attended = spread_attn[:, D:].reshape(seq_len, local_heads, HD)
        micro_out = inner_rows(attended, grad_mixed_full)

        def backward_block(sums_pair, block_index):
            key_sum, value_sum = sums_pair
            row_begin = block_index * block_rows
            query_block = lax.dynamic_slice_in_dim(query_rows, row_begin, block_rows, 0)
            grad_block = lax.dynamic_slice_in_dim(grad_attended, row_begin, block_rows, 0)
            scores = jnp.einsum(
                "qhd,khd->hqk", query_block, key_rows, preferred_element_type=jnp.float32
            )
            scores = jnp.where(block_mask(row_begin, block_rows, key_live)[None], scores, -1e30)
            weights_full = jnp.exp(scores - log_totals[block_index][..., None])
            grad_weights = jnp.einsum(
                "qhd,khd->hqk", grad_block, value_rows, preferred_element_type=jnp.float32
            )
            centre = jnp.sum(weights_full * grad_weights, axis=-1, keepdims=True)
            grad_scores = (weights_full * (grad_weights - centre)).astype(jnp.bfloat16)
            grad_query_block = jnp.einsum(
                "hqk,khd->qhd", grad_scores, key_rows, preferred_element_type=jnp.float32
            )
            key_sum = key_sum + jnp.einsum(
                "hqk,qhd->khd", grad_scores, query_block, preferred_element_type=jnp.float32
            )
            value_sum = value_sum + jnp.einsum(
                "hqk,qhd->khd",
                weights_full.astype(jnp.bfloat16),
                grad_block,
                preferred_element_type=jnp.float32,
            )
            return (
                (key_sum, value_sum),
                grad_query_block.astype(jnp.bfloat16).reshape(block_rows, head_cols),
            )

        zero_heads = jnp.zeros((seq_len, local_heads, HD), jnp.float32)
        (key_sum, value_sum), query_blocks = lax.scan(
            backward_block, (zero_heads, zero_heads), jnp.arange(block_count, dtype=jnp.int32)
        )
        grad_query = query_blocks.reshape(seq_len, head_cols)
        grad_key = key_sum.astype(jnp.bfloat16).reshape(seq_len, head_cols)
        grad_value = value_sum.astype(jnp.bfloat16).reshape(seq_len, head_cols)
        micro_query = inner_rows(normed_full, grad_query) * qk_scale
        micro_key = inner_rows(normed_full, grad_key)
        micro_value = inner_rows(normed_full, grad_value)
        query_bias_grad = jnp.sum(grad_query.astype(jnp.float32), axis=0) * qk_scale
        value_bias_grad = jnp.sum(grad_value.astype(jnp.float32), axis=0)
        grad_normed = lax.psum_scatter(
            (
                times_t(grad_query, query_full) * qk_scale
                + times_t(grad_key, key_full)
                + times_t(grad_value, value_full)
            ).astype(jnp.bfloat16),
            "mp",
            scatter_dimension=0,
            tiled=True,
        ).astype(jnp.float32)
        grad_joined = grad_mixed + norm_back(grad_normed, unit_one, scale_one, attn_gain)
        input_grads.append(grad_joined)
        micro_grads = (micro_query, micro_key, micro_value, micro_out, micro_up, micro_down)
        full_sums = tuple(map(jnp.add, full_sums, micro_grads))
        head_sums = (
            head_sums[0] + query_bias_grad,
            head_sums[1] + value_bias_grad,
            head_sums[2] + up_bias_grad,
        )
        row_sums = (
            row_sums[0] + jnp.sum(grad_mixed, axis=0),
            row_sums[1] + jnp.sum(grad_layer, axis=0),
            row_sums[2] + jnp.sum(grad_normed * unit_one, axis=0),
            row_sums[3] + jnp.sum(grad_normed, axis=0),
            row_sums[4] + jnp.sum(grad_normed_two * unit_two, axis=0),
            row_sums[5] + jnp.sum(grad_normed_two, axis=0),
            row_sums[6] + jnp.dot(picker.T, grad_joined, precision=precise),
        )
    weight_total = (
        lax.psum_scatter(
            full_sums[0].astype(jnp.bfloat16), "dp", scatter_dimension=0, tiled=True
        ).astype(jnp.float32),
        lax.psum_scatter(
            full_sums[1].astype(jnp.bfloat16), "dp", scatter_dimension=0, tiled=True
        ).astype(jnp.float32),
        lax.psum_scatter(
            full_sums[2].astype(jnp.bfloat16), "dp", scatter_dimension=0, tiled=True
        ).astype(jnp.float32),
        lax.psum_scatter(
            full_sums[3].astype(jnp.bfloat16), "dp", scatter_dimension=1, tiled=True
        ).astype(jnp.float32),
        lax.psum_scatter(
            full_sums[4].astype(jnp.bfloat16), "dp", scatter_dimension=0, tiled=True
        ).astype(jnp.float32),
        lax.psum_scatter(
            full_sums[5].astype(jnp.bfloat16), "dp", scatter_dimension=1, tiled=True
        ).astype(jnp.float32),
    )
    head_total = lax.psum((head_sums[0], head_sums[1], head_sums[2]), "dp")
    row_total = lax.psum(
        (row_sums[0], row_sums[1], row_sums[2], row_sums[3], row_sums[4], row_sums[5], row_sums[6]),
        ("dp", "mp"),
    )
    return (
        jnp.stack(outputs),
        jnp.stack(input_grads),
        row_total[6],
        weight_total[0],
        head_total[0],
        weight_total[1],
        weight_total[2],
        head_total[1],
        weight_total[3],
        row_total[0],
        weight_total[4],
        head_total[2],
        weight_total[5],
        row_total[1],
        row_total[2],
        row_total[3],
        row_total[4],
        row_total[5],
    )


def solution(mesh):
    in_specs = (
        P(None, ("dp", "mp"), None),
        P(None, "dp"),
        P(),
        P("dp", "mp"),
        P("mp"),
        P("dp", "mp"),
        P("dp", "mp"),
        P("mp"),
        P("mp", "dp"),
        P(),
        P("dp", "mp"),
        P("mp"),
        P("mp", "dp"),
        P(),
        P(),
        P(),
        P(),
        P(),
        P(None, ("dp", "mp"), None),
    )
    out_specs = (
        P(None, ("dp", "mp"), None),
        P(None, ("dp", "mp"), None),
        P(),
        P("dp", "mp"),
        P("mp"),
        P("dp", "mp"),
        P("dp", "mp"),
        P("mp"),
        P("mp", "dp"),
        P(),
        P("dp", "mp"),
        P("mp"),
        P("mp", "dp"),
        P(),
        P(),
        P(),
        P(),
        P(),
    )
    return jax.shard_map(shards, mesh=mesh, in_specs=in_specs, out_specs=out_specs, check_vma=False)
```

profile of v0, /device:TPU:1, one launch (start us, length us, event | category | flops | bytes accessed | tf_op | source)
XLA Modules:
  0.0 2053.1 jit_solution(16066606750939423374)
XLA Ops:
  17.3 23.1 %all-gather.21.cloned.1.call-done = bf16[2048,512]{1,0:T(8,128)(2,1)} async-done(((bf16[256,512]{1,0:T(8,128)(2,1)}), bf16[2048,512]{1,0:T(8,128)(2,1)}) %all-gather.21.cloned.1.call-update) | async-done | bytes 2097168 | tf_op jit(solution)/shard_map/all_gather | solution.py:141
  40.4 82.5 %all-gather.17.cloned.1.call-done = bf16[1024,2048]{1,0:T(8,128)(2,1)} async-done(((bf16[256,2048]{1,0:T(8,128)(2,1)}), bf16[1024,2048]{1,0:T(8,128)(2,1)}) %all-gather.17.cloned.1.call-update) | async-done | bytes 4194320 | tf_op jit(solution)/shard_map/all_gather | solution.py:151
  128.1 23.5 %all-gather.19.cloned.1.call-done = bf16[2048,512]{1,0:T(8,128)(2,1)} async-done(((bf16[256,512]{1,0:T(8,128)(2,1)}), bf16[2048,512]{1,0:T(8,128)(2,1)}) %all-gather.19.cloned.1.call-update) | async-done | bytes 2097168 | tf_op jit(solution)/shard_map/all_gather | solution.py:140
  156.9 24.4 %all-gather.23.cloned.1.call-done = bf16[2048,512]{1,0:T(8,128)(2,1)} async-done(((bf16[256,512]{1,0:T(8,128)(2,1)}), bf16[2048,512]{1,0:T(8,128)(2,1)}) %all-gather.23.cloned.1.call-update) | async-done | bytes 2097168 | tf_op jit(solution)/shard_map/all_gather | solution.py:142
  188.6 33.1 %while.56 = (s32[]{:T(128)}, bf16[2,512,512]{2,1,0:T(8,128)(2,1)}, f32[2,8,512]{2,1,0:T(8,128)S(1)}, s32[2]{0:T(128)S(1)}, bf16[1024,8,64]{0,2,1:T(8,128)(2,1)S(...) while((s32[]{:T(128)}, bf16[2,512,512]{2,1,0:T(8,128)(2,1)}, ...), condition=%wide.region_5.6_spmd.clone, body=%wide.region_2.5_spmd.clone.sunk | while | flops 1112807936 | bytes 62003432 | solution.py:180
  229.3 64.5 %all-gather.33.cloned.1.call-done = bf16[1024,2048]{1,0:T(8,128)(2,1)} async-done(((bf16[256,2048]{1,0:T(8,128)(2,1)}), bf16[1024,2048]{1,0:T(8,128)(2,1)}) %all-gather.33.cloned.1.call-update) | async-done | bytes 4194320 | tf_op jit(solution)/shard_map/all_gather | solution.py:151
  307.8 33.3 %while.57 = (s32[]{:T(128)}, bf16[2,512,512]{2,1,0:T(8,128)(2,1)}, f32[2,8,512]{2,1,0:T(8,128)S(1)}, s32[2]{0:T(128)S(1)}, bf16[1024,8,64]{0,2,1:T(8,128)(2,1)S(...) while((s32[]{:T(128)}, bf16[2,512,512]{2,1,0:T(8,128)(2,1)}, ...), condition=%wide.region_15.16_spmd.clone, body=%wide.region_12.15_spmd.clone.sunk | while | flops 1112807936 | bytes 62003432 | solution.py:180
  349.1 22.8 %reduce-scatter.15.cloned.1.call-done = bf16[256,2048]{1,0:T(8,128)(2,1)} async-done(((bf16[1024,2048]{1,0:T(8,128)(2,1)}), bf16[256,2048]{1,0:T(8,128)(2,1)}) %reduce-scatter.15.cloned.1.call-update) | async-done | bytes 1048592 | tf_op jit(solution)/shard_map/reduce_scatter | solution.py:184
  371.9 79.7 %reduce-scatter.19.cloned.1.call-done = bf16[256,2048]{1,0:T(8,128)(2,1)} async-done(((bf16[1024,2048]{1,0:T(8,128)(2,1)}), bf16[256,2048]{1,0:T(8,128)(2,1)}) %reduce-scatter.19.cloned.1.call-update) | async-done | bytes 1048592 | tf_op jit(solution)/shard_map/reduce_scatter | solution.py:184
  461.7 47.2 %all-gather.29.cloned.1.call-done = bf16[2048,2048]{1,0:T(8,128)(2,1)} async-done(((bf16[256,2048]{1,0:T(8,128)(2,1)}), bf16[2048,2048]{1,0:T(8,128)(2,1)}) %all-gather.29.cloned.1.call-update) | async-done | bytes 8388624 | tf_op jit(solution)/shard_map/all_gather | solution.py:144
  508.8 82.4 %all-gather.27.cloned.1.call-done = bf16[1024,2048]{1,0:T(8,128)(2,1)} async-done(((bf16[256,2048]{1,0:T(8,128)(2,1)}), bf16[1024,2048]{1,0:T(8,128)(2,1)}) %all-gather.27.cloned.1.call-update) | async-done | bytes 4194320 | tf_op jit(solution)/shard_map/all_gather | solution.py:193
  591.2 14.7 fusion.180
  605.9 66.8 %all-gather.41.cloned.1.call-done = bf16[1,1024,2048]{2,1,0:T(8,128)(2,1)} async-done(((bf16[1,256,2048]{2,1,0:T(8,128)(2,1)}), bf16[1,1024,2048]{2,1,0:T(8,128)(2,1)}) %all-gather.41.cloned.1.call-update) | async-done | bytes 4194320 | tf_op jit(solution)/shard_map/all_gather | solution.py:213
  672.7 56.7 %all-gather.31.cloned.1.call-done = bf16[2048,2048]{1,0:T(8,128)(2,1)} async-done(((bf16[2048,256]{1,0:T(8,128)(2,1)}), bf16[2048,2048]{1,0:T(8,128)(2,1)}) %all-gather.31.cloned.1.call-update) | async-done | bytes 8388624 | tf_op jit(solution)/shard_map/all_gather | solution.py:145
  729.3 18.8 convert_reduce_fusion.1
  750.2 13.0 convolution_convert_fusion.3
  763.2 48.0 %all-gather.35.cloned.1.call-done = bf16[1024,2048]{1,0:T(8,128)(2,1)} async-done(((bf16[256,2048]{1,0:T(8,128)(2,1)}), bf16[1024,2048]{1,0:T(8,128)(2,1)}) %all-gather.35.cloned.1.call-update) | async-done | bytes 4194320 | tf_op jit(solution)/shard_map/all_gather | solution.py:193
  811.3 14.6 fusion.181
  825.8 66.2 %all-gather.43.cloned.1.call-done = bf16[1,1024,2048]{2,1,0:T(8,128)(2,1)} async-done(((bf16[1,256,2048]{2,1,0:T(8,128)(2,1)}), bf16[1,1024,2048]{2,1,0:T(8,128)(2,1)}) %all-gather.43.cloned.1.call-update) | async-done | bytes 4194320 | tf_op jit(solution)/shard_map/all_gather | solution.py:213
  892.0 18.8 convert_reduce_fusion
  912.9 13.4 convolution_convert_fusion.2
  926.3 16.1 convolution_convert_fusion.4
  942.5 16.2 convolution_convert_fusion.6
  959.3 10.8 reduce-scatter.23.cloned.1.call-done
  970.1 79.5 %reduce-scatter.27.cloned.1.call-done = bf16[256,2048]{1,0:T(8,128)(2,1)} async-done(((bf16[1024,2048]{1,0:T(8,128)(2,1)}), bf16[256,2048]{1,0:T(8,128)(2,1)}) %reduce-scatter.27.cloned.1.call-update) | async-done | bytes 1048592 | tf_op jit(solution)/shard_map/reduce_scatter | solution.py:223
  1053.8 75.2 %reduce-scatter.21.cloned.1.call-done = bf16[256,2048]{1,0:T(8,128)(2,1)} async-done(((bf16[1024,2048]{1,0:T(8,128)(2,1)}), bf16[256,2048]{1,0:T(8,128)(2,1)}) %reduce-scatter.21.cloned.1.call-update) | async-done | bytes 1048592 | tf_op jit(solution)/shard_map/reduce_scatter | solution.py:205
  1129.1 79.5 %reduce-scatter.17.cloned.1.call-done = bf16[256,2048]{1,0:T(8,128)(2,1)} async-done(((bf16[1024,2048]{1,0:T(8,128)(2,1)}), bf16[256,2048]{1,0:T(8,128)(2,1)}) %reduce-scatter.17.cloned.1.call-update) | async-done | bytes 1048592 | tf_op jit(solution)/shard_map/reduce_scatter | solution.py:205
  1218.9 15.5 fusion.190
  1234.4 14.7 add_convert_fusion.1
  1249.2 17.9 fusion.124
  1267.1 21.3 %add_convert_fusion = bf16[2048,2048]{1,0:T(8,128)(2,1)} fusion(f32[2048,2048]{1,0:T(8,128)} %fusion.124, bf16[1,1024,2048]{2,1,0:T(8,128)(2,1)S(1)} %copy-done.106, f32[1024,2048]{1,0:T(8,128)} %fusion.181, f32[2048]{0:T(1024)S(1)} %convert_element_type.266), kind=kOutput, calls=%fused_computation.128 | convolution fusion | flops 8619294720 | bytes 37756928 | tf_op jit(solution)/shard_map/dot_general | solution.py:50
  1288.5 10.6 all-gather.39.cloned.1.call-done
  1306.4 122.1 %while.59 = (s32[]{:T(128)}, f32[1024,8,64]{0,2,1:T(8,128)}, f32[1024,8,64]{0,2,1:T(8,128)}, bf16[2,512,512]{1,2,0:T(8,128)(2,1)}, s32[2]{0:T(128)S(1)}, /*index...) while((s32[]{:T(128)}, f32[1024,8,64]{0,2,1:T(8,128)}, ...), condition=%wide.region_34.35_spmd.clone, body=%wide.region_32.34_spmd.clone.sunk | while | flops 2738100736 | bytes 252303984 | solution.py:268
  1320.1 14.8 multiply_reduce_fusion.9
  1337.1 10.5 multiply_convert_fusion.8
  1379.8 15.5 multiply_reduce_fusion.9
  1398.2 10.6 multiply_convert_fusion.8
  1438.5 122.9 %while.58 = (s32[]{:T(128)}, f32[1024,8,64]{0,2,1:T(8,128)}, f32[1024,8,64]{0,2,1:T(8,128)}, bf16[2,512,512]{1,2,0:T(8,128)(2,1)}, s32[2]{0:T(128)S(1)}, /*index...) while((s32[]{:T(128)}, f32[1024,8,64]{0,2,1:T(8,128)}, ...), condition=%wide.region_25.26_spmd.clone, body=%wide.region_23.25_spmd.clone.sunk | while | flops 2738100736 | bytes 252303984 | solution.py:268
  1452.1 15.3 multiply_reduce_fusion.8
  1470.3 11.2 multiply_convert_fusion.7
  1514.8 14.8 multiply_reduce_fusion.8
  1641.3 22.2 %all-reduce.1 = (f32[512]{0:T(512)}, f32[512]{0:T(512)}, f32[2048]{0:T(1024)}) all-reduce(f32[512]{0:T(512)S(1)} %add_multiply_fusion, f32[512]{0:T(512)S(1)} %add.506, f32[2048]{0:T(1024)S(1)} %add.510), channel_id=1, replica_groups=mesh['dp'=8,'mp'=4] {'dp'}, use_global_device_ids=true, to_apply=%region_42.43 | all-reduce | flops 3072 | bytes 24576 | tf_op jit(solution)/shard_map/psum | solution.py:327
  1667.2 35.3 %reduce-scatter.35.cloned.1.call-done = bf16[256,512]{1,0:T(8,128)(2,1)} async-done(((bf16[2048,512]{1,0:T(8,128)(2,1)}), bf16[256,512]{1,0:T(8,128)(2,1)}) %reduce-scatter.35.cloned.1.call-update) | async-done | bytes 262160 | tf_op jit(solution)/shard_map/reduce_scatter | solution.py:314
  1704.3 42.9 %reduce-scatter.37.cloned.1.call-done = bf16[512,256]{1,0:T(8,128)(2,1)} async-done(((bf16[512,2048]{1,0:T(8,128)(2,1)}), bf16[512,256]{1,0:T(8,128)(2,1)}) %reduce-scatter.37.cloned.1.call-update) | async-done | bytes 262160 | tf_op jit(solution)/shard_map/reduce_scatter | solution.py:317
  1749.0 77.2 %reduce-scatter.25.cloned.1.call-done = bf16[256,2048]{1,0:T(8,128)(2,1)} async-done(((bf16[1024,2048]{1,0:T(8,128)(2,1)}), bf16[256,2048]{1,0:T(8,128)(2,1)}) %reduce-scatter.25.cloned.1.call-update) | async-done | bytes 1048592 | tf_op jit(solution)/shard_map/reduce_scatter | solution.py:279
  1828.4 78.0 %reduce-scatter.29.cloned.1.call-done = bf16[256,2048]{1,0:T(8,128)(2,1)} async-done(((bf16[1024,2048]{1,0:T(8,128)(2,1)}), bf16[256,2048]{1,0:T(8,128)(2,1)}) %reduce-scatter.29.cloned.1.call-update) | async-done | bytes 1048592 | tf_op jit(solution)/shard_map/reduce_scatter | solution.py:279
  1916.6 41.8 %all-reduce = (f32[2048]{0:T(1024)}, f32[2048]{0:T(1024)}, f32[2048]{0:T(1024)}, f32[2048]{0:T(1024)}, f32[2048]{0:T(1024)}, /*index=5*/f32[2048]{0:T(1024)}) all-reduce(f32[2048]{0:T(1024)S(1)} %add.508, f32[2048]{0:T(1024)S(1)} %add.512, f32[2048]{0:T(1024)S(1)} %add.513, ...), channel_id=1, replica_groups=mesh['dp'=8,'mp'=4] {'dp','mp'}, use_global_device_ids=true, to_apply=%region_51.52 | all-reduce | flops 12288 | bytes 98304 | tf_op jit(solution)/shard_map/psum | solution.py:328
  1962.4 81.9 %all-reduce.4.cloned.1.call-done = f32[50,2048]{1,0:T(8,128)} async-done(((f32[50,2048]{1,0:T(8,128)}), f32[50,2048]{1,0:T(8,128)}) %all-reduce.4.cloned.1.call-update) | async-done | bytes 409616 | tf_op jit(solution)/shard_map/psum | solution.py:328
  (563 shorter events, 411.9 us)
Async XLA Ops:
  7.2 33.2 %all-gather.21.cloned.1.call-start = ((), (), s32[]{:S(2)}) async-start(), calls=%async_computation.16 | async-start | bytes 2359296 | tf_op jit(solution)/shard_map/all_gather | solution.py:141
  7.9 114.9 %all-gather.17.cloned.1.call-start = ((), (), s32[]{:S(2)}) async-start(), calls=%async_computation.14 | async-start | bytes 5242880 | tf_op jit(solution)/shard_map/all_gather | solution.py:151
  14.1 137.6 %all-gather.19.cloned.1.call-start = ((), (), s32[]{:S(2)}) async-start(), calls=%async_computation.15 | async-start | bytes 2359296 | tf_op jit(solution)/shard_map/all_gather | solution.py:140
  14.8 166.5 %all-gather.23.cloned.1.call-start = ((), (), s32[]{:S(2)}) async-start(), calls=%async_computation.17 | async-start | bytes 2359296 | tf_op jit(solution)/shard_map/all_gather | solution.py:142
  15.4 206.4 %all-gather.25.cloned.1.call-start = ((), (), s32[]{:S(2)}) async-start(), calls=%async_computation.18 | async-start | bytes 2359296 | tf_op jit(solution)/shard_map/all_gather | solution.py:143
  16.0 277.8 %all-gather.33.cloned.1.call-start = ((), (), s32[]{:S(2)}) async-start(), calls=%async_computation.24 | async-start | bytes 5242880 | tf_op jit(solution)/shard_map/all_gather | solution.py:151
  16.6 355.3 %reduce-scatter.15.cloned.1.call-start = ((), (), s32[]{:S(2)}) async-start(), calls=%async_computation.19 | async-start | bytes 5242880 | tf_op jit(solution)/shard_map/reduce_scatter | solution.py:184
  16.6 135.0 %copy-start.95 = (f32[512]{0:T(512)}, f32[512]{0:T(512)S(1)}, u32[]{:S(2)}) copy-start(f32[512]{0:T(512)S(1)} %convert_element_type.257) | copy-start | bytes 6148
  16.7 164.7 %copy-start.93 = (f32[512]{0:T(512)}, f32[512]{0:T(512)S(1)}, u32[]{:S(2)}) copy-start(f32[512]{0:T(512)S(1)} %convert_element_type.260) | copy-start | bytes 6148
  228.9 64.8 %copy-start.96 = (f32[512]{0:T(512)S(1)}, f32[512]{0:T(512)}, u32[]{:S(2)}) copy-start(f32[512]{0:T(512)} %copy-done.95) | copy-start | bytes 6148
  229.0 222.6 %reduce-scatter.19.cloned.1.call-start = ((), (), s32[]{:S(2)}) async-start(), calls=%async_computation.25 | async-start | bytes 5242880 | tf_op jit(solution)/shard_map/reduce_scatter | solution.py:184
  348.2 103.4 %copy-start.15 = (f32[256,2048]{1,0:T(8,128)S(1)}, f32[256,2048]{1,0:T(8,128)}, u32[]{:S(2)}) copy-start(f32[256,2048]{1,0:T(8,128)} %copy-done.14) | copy-start | bytes 6291460
  348.3 160.6 %all-gather.29.cloned.1.call-start = ((), (), s32[]{:S(2)}) async-start(), calls=%async_computation.21 | async-start | bytes 9437184 | tf_op jit(solution)/shard_map/all_gather | solution.py:144
  349.0 242.2 %all-gather.27.cloned.1.call-start = ((), (), s32[]{:S(2)}) async-start(), calls=%async_computation.20 | async-start | bytes 5242880 | tf_op jit(solution)/shard_map/all_gather | solution.py:193
  457.4 215.3 %all-gather.41.cloned.1.call-start = ((), (), s32[]{:S(2)}) async-start(), calls=%async_computation.41 | async-start | bytes 5242880 | tf_op jit(solution)/shard_map/all_gather | solution.py:213
  459.7 269.6 %all-gather.31.cloned.1.call-start = ((), (), s32[]{:S(2)}) async-start(), calls=%async_computation.22 | async-start | bytes 9437184 | tf_op jit(solution)/shard_map/all_gather | solution.py:145
  460.3 351.0 %all-gather.35.cloned.1.call-start = ((), (), s32[]{:S(2)}) async-start(), calls=%async_computation.26 | async-start | bytes 5242880 | tf_op jit(solution)/shard_map/all_gather | solution.py:193
  461.0 431.0 %all-gather.43.cloned.1.call-start = ((), (), s32[]{:S(2)}) async-start(), calls=%async_computation.42 | async-start | bytes 5242880 | tf_op jit(solution)/shard_map/all_gather | solution.py:213
  461.6 508.5 %reduce-scatter.23.cloned.1.call-start = ((), (), s32[]{:S(2)}) async-start(), calls=%async_computation.28 | async-start | bytes 5242880 | tf_op jit(solution)/shard_map/reduce_scatter | solution.py:223
  763.2 286.4 %reduce-scatter.27.cloned.1.call-start = ((), (), s32[]{:S(2)}) async-start(), calls=%async_computation.31 | async-start | bytes 5242880 | tf_op jit(solution)/shard_map/reduce_scatter | solution.py:223
  926.2 202.9 %reduce-scatter.21.cloned.1.call-start = ((), (), s32[]{:S(2)}) async-start(), calls=%async_computation.27 | async-start | bytes 5242880 | tf_op jit(solution)/shard_map/reduce_scatter | solution.py:205
  942.4 266.2 %reduce-scatter.17.cloned.1.call-start = ((), (), s32[]{:S(2)}) async-start(), calls=%async_computation.23 | async-start | bytes 5242880 | tf_op jit(solution)/shard_map/reduce_scatter | solution.py:205
  958.6 91.0 %copy-start.22 = (f32[256,2048]{1,0:T(8,128)S(1)}, f32[256,2048]{1,0:T(8,128)}, u32[]{:S(2)}) copy-start(f32[256,2048]{1,0:T(8,128)} %copy-done.21) | copy-start | bytes 6291460
  958.7 91.0 %copy-start.61 = (f32[2048]{0:T(1024)S(1)}, f32[2048]{0:T(1024)}, u32[]{:S(2)}) copy-start(f32[2048]{0:T(1024)} %param.43) | copy-start | bytes 24580
  958.7 91.0 %copy-start.73 = (f32[256]{0:T(256)S(1)}, f32[256]{0:T(256)}, u32[]{:S(2)}) copy-start(f32[256]{0:T(256)} %copy-done.72) | copy-start | bytes 3076
  958.7 91.0 %copy-start.75 = (f32[256]{0:T(256)S(1)}, f32[256]{0:T(256)}, u32[]{:S(2)}) copy-start(f32[256]{0:T(256)} %copy-done.74) | copy-start | bytes 3076
  958.7 91.0 %copy-start.81 = (f32[256]{0:T(256)S(1)}, f32[256]{0:T(256)}, u32[]{:S(2)}) copy-start(f32[256]{0:T(256)} %copy-done.80) | copy-start | bytes 3076
  958.7 91.0 %copy-start.83 = (f32[256]{0:T(256)S(1)}, f32[256]{0:T(256)}, u32[]{:S(2)}) copy-start(f32[256]{0:T(256)} %copy-done.82) | copy-start | bytes 3076
  958.7 340.3 %all-gather.39.cloned.1.call-start = ((), (), s32[]{:S(2)}) async-start(), calls=%async_computation.32 | async-start | bytes 5242880 | tf_op jit(solution)/shard_map/all_gather | solution.py:227
  1217.6 213.4 %all-gather.37.cloned.1.call-start = ((), (), s32[]{:S(2)}) async-start(), calls=%async_computation.29 | async-start | bytes 5242880 | tf_op jit(solution)/shard_map/all_gather | solution.py:227
  1218.8 413.9 %reduce-scatter.39.cloned.1.call-start = ((), (), s32[]{:S(2)}) async-start(), calls=%async_computation.39 | async-start | bytes 9437184 | tf_op jit(solution)/shard_map/reduce_scatter | solution.py:320
  1249.1 386.4 %reduce-scatter.41.cloned.1.call-start = ((), (), s32[]{:S(2)}) async-start(), calls=%async_computation.40 | async-start | bytes 9437184 | tf_op jit(solution)/shard_map/reduce_scatter | solution.py:323
  1288.4 375.1 %reduce-scatter.31.cloned.1.call-start = ((), (), s32[]{:S(2)}) async-start(), calls=%async_computation.35 | async-start | bytes 2359296 | tf_op jit(solution)/shard_map/reduce_scatter | solution.py:308
  1572.0 93.3 %reduce-scatter.33.cloned.1.call-start = ((), (), s32[]{:S(2)}) async-start(), calls=%async_computation.36 | async-start | bytes 2359296 | tf_op jit(solution)/shard_map/reduce_scatter | solution.py:311
  1582.5 119.9 %reduce-scatter.35.cloned.1.call-start = ((), (), s32[]{:S(2)}) async-start(), calls=%async_computation.37 | async-start | bytes 2359296 | tf_op jit(solution)/shard_map/reduce_scatter | solution.py:314
  1593.3 153.9 %reduce-scatter.37.cloned.1.call-start = ((), (), s32[]{:S(2)}) async-start(), calls=%async_computation.38 | async-start | bytes 2359296 | tf_op jit(solution)/shard_map/reduce_scatter | solution.py:317
  1601.9 224.3 %reduce-scatter.25.cloned.1.call-start = ((), (), s32[]{:S(2)}) async-start(), calls=%async_computation.30 | async-start | bytes 5242880 | tf_op jit(solution)/shard_map/reduce_scatter | solution.py:279
  1614.4 292.1 %reduce-scatter.29.cloned.1.call-start = ((), (), s32[]{:S(2)}) async-start(), calls=%async_computation.33 | async-start | bytes 5242880 | tf_op jit(solution)/shard_map/reduce_scatter | solution.py:279
  1627.5 416.8 %all-reduce.4.cloned.1.call-start = ((), (), s32[]{:S(2)}) async-start(), calls=%async_computation.34 | async-start | bytes 917504 | tf_op jit(solution)/shard_map/psum | solution.py:328
  1635.5 190.7 %copy-start.16 = (f32[256,2048]{1,0:T(8,128)S(1)}, f32[256,2048]{1,0:T(8,128)}, u32[]{:S(2)}) copy-start(f32[256,2048]{1,0:T(8,128)} %copy-done.14) | copy-start | bytes 6291460
  1635.5 190.7 %copy-start.59 = (f32[2048]{0:T(1024)S(1)}, f32[2048]{0:T(1024)}, u32[]{:S(2)}) copy-start(f32[2048]{0:T(1024)} %param.41) | copy-start | bytes 24580
  1635.5 190.7 %copy-start.69 = (f32[256]{0:T(256)S(1)}, f32[256]{0:T(256)}, u32[]{:S(2)}) copy-start(f32[256]{0:T(256)} %copy-done.68) | copy-start | bytes 3076
  1635.5 190.7 %copy-start.77 = (f32[256]{0:T(256)S(1)}, f32[256]{0:T(256)}, u32[]{:S(2)}) copy-start(f32[256]{0:T(256)} %copy-done.76) | copy-start | bytes 3076
  1638.5 268.0 %copy-start.71 = (f32[256]{0:T(256)S(1)}, f32[256]{0:T(256)}, u32[]{:S(2)}) copy-start(f32[256]{0:T(256)} %copy-done.70) | copy-start | bytes 3076
  1638.5 268.0 %copy-start.79 = (f32[256]{0:T(256)S(1)}, f32[256]{0:T(256)}, u32[]{:S(2)}) copy-start(f32[256]{0:T(256)} %copy-done.78) | copy-start | bytes 3076
  1828.4 83.2 %copy-start.85 = (s32[256]{0:T(256)S(1)}, s32[256]{0:T(256)}, u32[]{:S(2)}) copy-start(s32[256]{0:T(256)} %copy-done.84) | copy-start | bytes 3076
  1912.6 45.8 %copy-start.29 = (f32[256,2048]{1,0:T(8,128)S(1)}, f32[256,2048]{1,0:T(8,128)}, u32[]{:S(2)}) copy-start(f32[256,2048]{1,0:T(8,128)} %copy-done.28) | copy-start | bytes 6291460
  1958.4 87.7 %copy-start.1 = (f32[50,2048]{1,0:T(8,128)S(1)}, f32[50,2048]{1,0:T(8,128)}, u32[]{:S(2)}) copy-start(f32[50,2048]{1,0:T(8,128)} %param.29) | copy-start | bytes 1228804
  (133 other events, 852.0 us)
Sparse Core Ops, SparseCore 0:
  9.9 30.3 all-gather.20
  42.5 80.3 all-gather.16
  124.8 26.8 all-gather.18
  153.4 27.8 all-gather.22
  183.1 28.1 all-gather.24
  213.3 80.4 all-gather.32
  296.6 75.2 reduce-scatter.14
  374.3 77.2 reduce-scatter.18
  453.5 55.2 all-gather.28
  510.8 80.3 all-gather.26
  593.3 79.2 all-gather.40
  674.4 54.8 all-gather.30
  730.9 80.3 all-gather.34
  812.7 79.2 all-gather.42
  894.8 75.3 reduce-scatter.22
  972.4 77.2 reduce-scatter.26
  1051.8 77.2 reduce-scatter.20
  1131.3 77.2 reduce-scatter.16
  1217.7 81.2 all-gather.38
  1300.4 79.2 all-gather.36
  1383.2 69.7 reduce-scatter.38
  1456.9 71.2 reduce-scatter.40
  1572.2 40.9 reduce-scatter.30
  1616.6 41.3 reduce-scatter.32
  1661.3 41.1 reduce-scatter.34
  1706.0 41.2 reduce-scatter.36
  1749.4 76.7 reduce-scatter.24
  1829.2 77.2 reduce-scatter.28
  1916.7 127.5 all-reduce.3
where the time goes:
time: 2060 us; the launch traced here: 2050 us
  waiting for transfers between devices  1260 us (61%)
  matrix products  513 us (25%)
  other arithmetic  122 us (6%)
  blocking collectives  64 us (3%)
  local copies, waits for them, and re-layouts  56.1 us (3%)
    reduce_scatter x2, waiting for transfers between devices, shards(): lax.psum_scatter((times_t(grad_query, query_full) * qk_scale + times_t(gr...  155 us
    reduce_scatter x2, waiting for transfers between devices, shards(): lax.psum_scatter(dense(active, down_full).astype(jnp.bfloat16), 'mp', sca...  155 us
    all_gather x2, waiting for transfers between devices, shards(): lax.all_gather(normed.astype(jnp.bfloat16), 'mp', axis=0, tiled=True)  147 us
    all_gather x2, waiting for transfers between devices, shards(): mlp_shard_rows = lax.all_gather(grad_rows, 'mp', axis=0, tiled=True)  133 us
    all_gather x2, waiting for transfers between devices, shards(): lax.all_gather(normed_two.astype(jnp.bfloat16), 'mp', axis=0, tiled=True)  130 us
    dot_general x12, matrix products, dense(): return jnp.dot(left_side, right_side, preferred_element_type=jnp.float32)  105 us
    reduce_scatter x2, waiting for transfers between devices, shards(): lax.psum_scatter(dense(attended, out_full).astype(jnp.bfloat16), 'mp', sc...  103 us
    dot_general x12, matrix products, times_t(): lax.dot_general(left_side, right_side, (((1,), (1,)), ((), ())), preferre...  101 us
  transfers between devices with their start and end apart: 29, of which 23 were waited for; matrix products, arithmetic and copies ran while one was open for 31% of the time, Pallas kernels for 0%

commit v1 on v0

--- a/solution.py
+++ b/solution.py
@@ -210,7 +210,14 @@
         outputs.append(layer_rows.astype(jnp.bfloat16))
         grad_rows = cotangent[micro_step]
         grad_layer = grad_rows.astype(jnp.float32)
-        mlp_shard_rows = lax.all_gather(grad_rows, "mp", axis=0, tiled=True)
+        ring = [grad_rows]
+        for hop in range(3):
+            ring.append(lax.ppermute(ring[-1], "mp", [(dev, (dev + 1) % 4) for dev in range(4)]))
+        mlp_shard_rows = jnp.roll(
+            jnp.concatenate(ring[::-1], axis=0),
+            (lax.axis_index("mp") + 1) * ring[0].shape[0],
+            axis=0,
+        )
         mlp_up_value = dense(normed_two_full, up_full) + bias_up
         grad_active = times_t(mlp_shard_rows, down_full)
         mlp_grad_up = (grad_active * gelu_slope(mlp_up_value)).astype(jnp.bfloat16)

time: 2060 us -> 1950 us (0.947)
  waiting for transfers between devices: 1260 us -> 1150 us
  matrix products: 513 us -> 466 us
  other arithmetic: 122 us -> 157 us
  starting transfers between devices: 2.06 us -> 29.2 us
    ppermute x0 -> x6, waiting for transfers between devices: none -> 139 us  [shards(): lax.ppermute(ring[-1], 'mp', [(dev, (dev + 1) % 4) for dev in range(4)])]
    all_gather x2 -> x0, waiting for transfers between devices: 133 us -> none  [shards(): mlp_shard_rows = lax.all_gather(grad_rows, 'mp', axis=0, tiled=True)]
    all_gather x2, waiting for transfers between devices: 130 us -> 52 us  [shards(): lax.all_gather(normed_two.astype(jnp.bfloat16), 'mp', axis=0, tiled=True)]
    all_gather x2, waiting for transfers between devices: 10.6 us -> 80.2 us  [shards(): lax.all_gather(grad_mixed.astype(jnp.bfloat16), 'mp', axis=0, tiled=True)]
    all_gather x1, waiting for transfers between devices: 47.2 us -> 0.02 us  [shards(): lax.all_gather(up_weight, 'dp', axis=0, tiled=True)]
    reduce_scatter x1, waiting for transfers between devices: 42.9 us -> 0.01 us  [shards(): lax.psum_scatter(full_sums[3].astype(jnp.bfloat16), 'dp', scatter_dimensi...]
    reduce_scatter x1, waiting for transfers between devices: 0.01 us -> 41.3 us  [shards(): lax.psum_scatter(full_sums[1].astype(jnp.bfloat16), 'dp', scatter_dimensi...]
    reduce_scatter x1, waiting for transfers between devices: 35.3 us -> 0.01 us  [shards(): lax.psum_scatter(full_sums[2].astype(jnp.bfloat16), 'dp', scatter_dimensi...]
  transfers between devices with their start and end apart: 29 -> 33, of which waited for: 23 -> 24; matrix products, arithmetic and copies ran while one was open for 31% -> 32% of each run, Pallas kernels for 0% -> 0%
where the time goes in v1:
time: 1950 us; the launch traced here: 1940 us
  waiting for transfers between devices  1150 us (59%)
  matrix products  466 us (24%)
  other arithmetic  157 us (8%)
  blocking collectives  64.1 us (3%)
  local copies, waits for them, and re-layouts  39.8 us (2%)
  starting transfers between devices  29.2 us (1%)
    reduce_scatter x2, waiting for transfers between devices, shards(): lax.psum_scatter((times_t(grad_query, query_full) * qk_scale + times_t(gr...  155 us
    reduce_scatter x2, waiting for transfers between devices, shards(): lax.psum_scatter(dense(active, down_full).astype(jnp.bfloat16), 'mp', sca...  155 us
    all_gather x2, waiting for transfers between devices, shards(): lax.all_gather(normed.astype(jnp.bfloat16), 'mp', axis=0, tiled=True)  148 us
    ppermute x6, waiting for transfers between devices, shards(): lax.ppermute(ring[-1], 'mp', [(dev, (dev + 1) % 4) for dev in range(4)])  139 us
    dot_general x12, matrix products, dense(): return jnp.dot(left_side, right_side, preferred_element_type=jnp.float32)  105 us
    reduce_scatter x2, waiting for transfers between devices, shards(): lax.psum_scatter(dense(attended, out_full).astype(jnp.bfloat16), 'mp', sc...  104 us
    dot_general x12, matrix products, inner_rows(): lax.dot_general(left_side, right_side, (((0,), (0,)), ((), ())), preferre...  103 us
    dot_general x12, matrix products, times_t(): lax.dot_general(left_side, right_side, (((1,), (1,)), ((), ())), preferre...  95.2 us
  transfers between devices with their start and end apart: 33, of which 24 were waited for; matrix products, arithmetic and copies ran while one was open for 32% of the time, Pallas kernels for 0%

profile of v1, /device:TPU:1, one launch (start us, length us, event | category | flops | bytes accessed | tf_op | source)
XLA Modules:
  0.0 1937.9 jit_solution(14688139732212548663)
XLA Ops:
  17.3 23.1 %all-gather.17.cloned.1.call-done = bf16[2048,512]{1,0:T(8,128)(2,1)} async-done(((bf16[256,512]{1,0:T(8,128)(2,1)}), bf16[2048,512]{1,0:T(8,128)(2,1)}) %all-gather.17.cloned.1.call-update) | async-done | bytes 2097168 | tf_op jit(solution)/shard_map/all_gather | solution.py:141
  40.4 82.5 %all-gather.13.cloned.1.call-done = bf16[1024,2048]{1,0:T(8,128)(2,1)} async-done(((bf16[256,2048]{1,0:T(8,128)(2,1)}), bf16[1024,2048]{1,0:T(8,128)(2,1)}) %all-gather.13.cloned.1.call-update) | async-done | bytes 4194320 | tf_op jit(solution)/shard_map/all_gather | solution.py:151
  128.1 23.5 %all-gather.19.cloned.1.call-done = bf16[2048,512]{1,0:T(8,128)(2,1)} async-done(((bf16[256,512]{1,0:T(8,128)(2,1)}), bf16[2048,512]{1,0:T(8,128)(2,1)}) %all-gather.19.cloned.1.call-update) | async-done | bytes 2097168 | tf_op jit(solution)/shard_map/all_gather | solution.py:142
  157.9 23.4 %all-gather.15.cloned.1.call-done = bf16[2048,512]{1,0:T(8,128)(2,1)} async-done(((bf16[256,512]{1,0:T(8,128)(2,1)}), bf16[2048,512]{1,0:T(8,128)(2,1)}) %all-gather.15.cloned.1.call-update) | async-done | bytes 2097168 | tf_op jit(solution)/shard_map/all_gather | solution.py:140
  187.6 33.4 %while.56 = (s32[]{:T(128)}, bf16[2,512,512]{2,1,0:T(8,128)(2,1)}, f32[2,8,512]{2,1,0:T(8,128)S(1)}, s32[2]{0:T(128)S(1)}, bf16[1024,8,64]{0,2,1:T(8,128)(2,1)S(...) while((s32[]{:T(128)}, bf16[2,512,512]{2,1,0:T(8,128)(2,1)}, ...), condition=%wide.region_5.6_spmd.clone, body=%wide.region_2.5_spmd.clone.sunk | while | flops 1112807936 | bytes 62003432 | solution.py:180
  228.6 65.1 %all-gather.29.cloned.1.call-done = bf16[1024,2048]{1,0:T(8,128)(2,1)} async-done(((bf16[256,2048]{1,0:T(8,128)(2,1)}), bf16[1024,2048]{1,0:T(8,128)(2,1)}) %all-gather.29.cloned.1.call-update) | async-done | bytes 4194320 | tf_op jit(solution)/shard_map/all_gather | solution.py:151
  307.1 33.0 %while.57 = (s32[]{:T(128)}, bf16[2,512,512]{2,1,0:T(8,128)(2,1)}, f32[2,8,512]{2,1,0:T(8,128)S(1)}, s32[2]{0:T(128)S(1)}, bf16[1024,8,64]{0,2,1:T(8,128)(2,1)S(...) while((s32[]{:T(128)}, bf16[2,512,512]{2,1,0:T(8,128)(2,1)}, ...), condition=%wide.region_15.16_spmd.clone, body=%wide.region_12.15_spmd.clone.sunk | while | flops 1112807936 | bytes 62003432 | solution.py:180
  348.1 23.8 %reduce-scatter.15.cloned.1.call-done = bf16[256,2048]{1,0:T(8,128)(2,1)} async-done(((bf16[1024,2048]{1,0:T(8,128)(2,1)}), bf16[256,2048]{1,0:T(8,128)(2,1)}) %reduce-scatter.15.cloned.1.call-update) | async-done | bytes 1048592 | tf_op jit(solution)/shard_map/reduce_scatter | solution.py:184
  371.9 79.7 %reduce-scatter.19.cloned.1.call-done = bf16[256,2048]{1,0:T(8,128)(2,1)} async-done(((bf16[1024,2048]{1,0:T(8,128)(2,1)}), bf16[256,2048]{1,0:T(8,128)(2,1)}) %reduce-scatter.19.cloned.1.call-update) | async-done | bytes 1048592 | tf_op jit(solution)/shard_map/reduce_scatter | solution.py:184
  461.4 22.9 %collective-permute-done.3 = bf16[256,2048]{1,0:T(8,128)(2,1)S(1)} collective-permute-done((bf16[256,2048]{1,0:T(8,128)(2,1)S(1)}, bf16[256,2048]{1,0:T(8,128)(2,1)S(1)}, u32[]{:S(2)}, u32[]{:S(2)}) %collective-permute-start.3) | collective-permute-done | bytes 1048608 | tf_op jit(solution)/shard_map/ppermute | solution.py:215
  484.3 22.5 %collective-permute-done = bf16[256,2048]{1,0:T(8,128)(2,1)S(1)} collective-permute-done((bf16[256,2048]{1,0:T(8,128)(2,1)S(1)}, bf16[256,2048]{1,0:T(8,128)(2,1)S(1)}, u32[]{:S(2)}, u32[]{:S(2)}) %collective-permute-start) | collective-permute-done | bytes 1048608 | tf_op jit(solution)/shard_map/ppermute | solution.py:215
  506.7 28.2 %collective-permute-done.4 = bf16[256,2048]{1,0:T(8,128)(2,1)} collective-permute-done((bf16[256,2048]{1,0:T(8,128)(2,1)S(1)}, bf16[256,2048]{1,0:T(8,128)(2,1)}, u32[]{:S(2)}, u32[]{:S(2)}) %collective-permute-start.4) | collective-permute-done | bytes 1048608 | tf_op jit(solution)/shard_map/ppermute | solution.py:215
  540.7 39.2 %collective-permute-done.1 = bf16[256,2048]{1,0:T(8,128)(2,1)} collective-permute-done((bf16[256,2048]{1,0:T(8,128)(2,1)S(1)}, bf16[256,2048]{1,0:T(8,128)(2,1)}, u32[]{:S(2)}, u32[]{:S(2)}) %collective-permute-start.1) | collective-permute-done | bytes 1048608 | tf_op jit(solution)/shard_map/ppermute | solution.py:215
  579.9 18.5 collective-permute-start.2
  598.4 26.4 %collective-permute-done.5 = bf16[256,2048]{1,0:T(8,128)(2,1)} collective-permute-done((bf16[256,2048]{1,0:T(8,128)(2,1)}, bf16[256,2048]{1,0:T(8,128)(2,1)}, u32[]{:S(2)}, u32[]{:S(2)}) %collective-permute-start.5) | collective-permute-done | bytes 1048608 | tf_op jit(solution)/shard_map/ppermute | solution.py:215
  624.8 15.0 fusion.125
  639.9 18.8 all-gather.31.cloned.1.call-done
  658.8 14.7 fusion.186
  673.5 41.6 %all-gather.27.cloned.1.call-done = bf16[2048,2048]{1,0:T(8,128)(2,1)} async-done(((bf16[2048,256]{1,0:T(8,128)(2,1)}), bf16[2048,2048]{1,0:T(8,128)(2,1)}) %all-gather.27.cloned.1.call-update) | async-done | bytes 8388624 | tf_op jit(solution)/shard_map/all_gather | solution.py:145
  715.1 18.9 convert_reduce_fusion
  747.6 16.7 fusion.132
  764.3 33.2 %all-gather.23.cloned.1.call-done = bf16[1024,2048]{1,0:T(8,128)(2,1)} async-done(((bf16[256,2048]{1,0:T(8,128)(2,1)}), bf16[1024,2048]{1,0:T(8,128)(2,1)}) %all-gather.23.cloned.1.call-update) | async-done | bytes 4194320 | tf_op jit(solution)/shard_map/all_gather | solution.py:193
  797.5 14.7 fusion.185
  812.2 18.2 convert_reduce_fusion.1
  842.9 16.3 convolution_convert_fusion.4
  859.2 16.1 convolution_convert_fusion.6
  876.0 78.7 %reduce-scatter.23.cloned.1.call-done = bf16[256,2048]{1,0:T(8,128)(2,1)} async-done(((bf16[1024,2048]{1,0:T(8,128)(2,1)}), bf16[256,2048]{1,0:T(8,128)(2,1)}) %reduce-scatter.23.cloned.1.call-update) | async-done | bytes 1048592 | tf_op jit(solution)/shard_map/reduce_scatter | solution.py:230
  958.7 75.4 %reduce-scatter.21.cloned.1.call-done = bf16[256,2048]{1,0:T(8,128)(2,1)} async-done(((bf16[1024,2048]{1,0:T(8,128)(2,1)}), bf16[256,2048]{1,0:T(8,128)(2,1)}) %reduce-scatter.21.cloned.1.call-update) | async-done | bytes 1048592 | tf_op jit(solution)/shard_map/reduce_scatter | solution.py:205
  1034.1 79.5 %reduce-scatter.17.cloned.1.call-done = bf16[256,2048]{1,0:T(8,128)(2,1)} async-done(((bf16[1024,2048]{1,0:T(8,128)(2,1)}), bf16[256,2048]{1,0:T(8,128)(2,1)}) %reduce-scatter.17.cloned.1.call-update) | async-done | bytes 1048592 | tf_op jit(solution)/shard_map/reduce_scatter | solution.py:205
  1124.0 17.6 fusion.173
  1141.6 21.4 %add_convert_fusion = bf16[2048,2048]{1,0:T(8,128)(2,1)} fusion(f32[2048,2048]{1,0:T(8,128)} %fusion.173, bf16[1024,2048]{1,0:T(8,128)(2,1)S(1)} %copy-done.43, f32[1024,2048]{1,0:T(8,128)} %fusion.185, f32[2048]{0:T(1024)S(1)} %convert_element_type.266), kind=kOutput, calls=%fused_computation.128 | convolution fusion | flops 8619294720 | bytes 37756928 | tf_op jit(solution)/shard_map/dot_general | solution.py:50
  1163.1 16.1 fusion.195
  1179.2 14.6 add_convert_fusion.1
  1215.0 69.9 %all-gather.35.cloned.1.call-done = bf16[1024,2048]{1,0:T(8,128)(2,1)} async-done(((bf16[256,2048]{1,0:T(8,128)(2,1)}), bf16[1024,2048]{1,0:T(8,128)(2,1)}) %all-gather.35.cloned.1.call-update) | async-done | bytes 4194320 | tf_op jit(solution)/shard_map/all_gather | solution.py:234
  1293.1 96.2 %while.58 = (s32[]{:T(128)}, f32[1024,8,64]{0,2,1:T(8,128)}, f32[1024,8,64]{0,2,1:T(8,128)}, bf16[2,512,512]{1,2,0:T(8,128)(2,1)}, s32[2]{0:T(128)S(1)}, /*index...) while((s32[]{:T(128)}, f32[1024,8,64]{0,2,1:T(8,128)}, ...), condition=%wide.region_25.27_spmd.clone, body=%wide.region_23.26_spmd.clone.sunk | while | flops 2738100736 | bytes 193583536 | solution.py:275
  1318.0 10.8 multiply_convert_fusion.7
  1354.4 10.6 multiply_reduce_fusion.8
  1365.0 11.9 multiply_convert_fusion.7
  1396.9 94.4 %while.59 = (s32[]{:T(128)}, f32[1024,8,64]{0,2,1:T(8,128)}, f32[1024,8,64]{0,2,1:T(8,128)}, bf16[2,512,512]{1,2,0:T(8,128)(2,1)}, s32[2]{0:T(128)S(1)}, /*index...) while((s32[]{:T(128)}, f32[1024,8,64]{0,2,1:T(8,128)}, ...), condition=%wide.region_34.36_spmd.clone, body=%wide.region_32.35_spmd.clone.sunk | while | flops 2738100736 | bytes 193583536 | solution.py:275
  1421.4 10.6 multiply_convert_fusion.8
  1457.5 10.8 multiply_reduce_fusion.9
  1468.3 10.6 multiply_convert_fusion.8
  1562.7 22.3 %all-reduce.1 = (f32[512]{0:T(512)}, f32[512]{0:T(512)}, f32[2048]{0:T(1024)}) all-reduce(f32[512]{0:T(512)S(1)} %add_multiply_fusion, f32[512]{0:T(512)S(1)} %add.519, f32[2048]{0:T(1024)S(1)} %add.523), channel_id=1, replica_groups=mesh['dp'=8,'mp'=4] {'dp'}, use_global_device_ids=true, to_apply=%region_42.44 | all-reduce | flops 3072 | bytes 24576 | tf_op jit(solution)/shard_map/psum | solution.py:334
  1590.4 41.3 %reduce-scatter.33.cloned.1.call-done = bf16[256,512]{1,0:T(8,128)(2,1)} async-done(((bf16[2048,512]{1,0:T(8,128)(2,1)}), bf16[256,512]{1,0:T(8,128)(2,1)}) %reduce-scatter.33.cloned.1.call-update) | async-done | bytes 262160 | tf_op jit(solution)/shard_map/reduce_scatter | solution.py:318
  1633.5 77.3 %reduce-scatter.25.cloned.1.call-done = bf16[256,2048]{1,0:T(8,128)(2,1)} async-done(((bf16[1024,2048]{1,0:T(8,128)(2,1)}), bf16[256,2048]{1,0:T(8,128)(2,1)}) %reduce-scatter.25.cloned.1.call-update) | async-done | bytes 1048592 | tf_op jit(solution)/shard_map/reduce_scatter | solution.py:286
  1713.1 77.9 %reduce-scatter.29.cloned.1.call-done = bf16[256,2048]{1,0:T(8,128)(2,1)} async-done(((bf16[1024,2048]{1,0:T(8,128)(2,1)}), bf16[256,2048]{1,0:T(8,128)(2,1)}) %reduce-scatter.29.cloned.1.call-update) | async-done | bytes 1048592 | tf_op jit(solution)/shard_map/reduce_scatter | solution.py:286
  1801.1 41.8 %all-reduce = (f32[2048]{0:T(1024)}, f32[2048]{0:T(1024)}, f32[2048]{0:T(1024)}, f32[2048]{0:T(1024)}, f32[2048]{0:T(1024)}, /*index=5*/f32[2048]{0:T(1024)}) all-reduce(f32[2048]{0:T(1024)S(1)} %add.521, f32[2048]{0:T(1024)S(1)} %add.525, f32[2048]{0:T(1024)S(1)} %add.526, ...), channel_id=1, replica_groups=mesh['dp'=8,'mp'=4] {'dp','mp'}, use_global_device_ids=true, to_apply=%region_51.53 | all-reduce | flops 12288 | bytes 98304 | tf_op jit(solution)/shard_map/psum | solution.py:335
  1846.9 81.9 %all-reduce.4.cloned.1.call-done = f32[50,2048]{1,0:T(8,128)} async-done(((f32[50,2048]{1,0:T(8,128)}), f32[50,2048]{1,0:T(8,128)}) %all-reduce.4.cloned.1.call-update) | async-done | bytes 409616 | tf_op jit(solution)/shard_map/psum | solution.py:335
  (520 shorter events, 422.8 us)
Async XLA Ops:
  7.2 33.2 %all-gather.17.cloned.1.call-start = ((), (), s32[]{:S(2)}) async-start(), calls=%async_computation.16 | async-start | bytes 2359296 | tf_op jit(solution)/shard_map/all_gather | solution.py:141
  7.9 114.9 %all-gather.13.cloned.1.call-start = ((), (), s32[]{:S(2)}) async-start(), calls=%async_computation.14 | async-start | bytes 5242880 | tf_op jit(solution)/shard_map/all_gather | solution.py:151
  14.1 137.6 %all-gather.19.cloned.1.call-start = ((), (), s32[]{:S(2)}) async-start(), calls=%async_computation.17 | async-start | bytes 2359296 | tf_op jit(solution)/shard_map/all_gather | solution.py:142
  14.8 166.5 %all-gather.15.cloned.1.call-start = ((), (), s32[]{:S(2)}) async-start(), calls=%async_computation.15 | async-start | bytes 2359296 | tf_op jit(solution)/shard_map/all_gather | solution.py:140
  15.4 205.6 %all-gather.21.cloned.1.call-start = ((), (), s32[]{:S(2)}) async-start(), calls=%async_computation.18 | async-start | bytes 2359296 | tf_op jit(solution)/shard_map/all_gather | solution.py:143
  16.0 277.7 %all-gather.29.cloned.1.call-start = ((), (), s32[]{:S(2)}) async-start(), calls=%async_computation.24 | async-start | bytes 5242880 | tf_op jit(solution)/shard_map/all_gather | solution.py:151
  16.6 355.3 %reduce-scatter.15.cloned.1.call-start = ((), (), s32[]{:S(2)}) async-start(), calls=%async_computation.19 | async-start | bytes 5242880 | tf_op jit(solution)/shard_map/reduce_scatter | solution.py:184
  17.2 164.1 %copy-start.95 = (f32[512]{0:T(512)}, f32[512]{0:T(512)S(1)}, u32[]{:S(2)}) copy-start(f32[512]{0:T(512)S(1)} %convert_element_type.257) | copy-start | bytes 6148
  17.2 134.4 %copy-start.97 = (f32[512]{0:T(512)}, f32[512]{0:T(512)S(1)}, u32[]{:S(2)}) copy-start(f32[512]{0:T(512)S(1)} %convert_element_type.260) | copy-start | bytes 6148
  228.4 223.2 %reduce-scatter.19.cloned.1.call-start = ((), (), s32[]{:S(2)}) async-start(), calls=%async_computation.25 | async-start | bytes 5242880 | tf_op jit(solution)/shard_map/reduce_scatter | solution.py:184
  347.2 104.4 %copy-start.8 = (f32[256,2048]{1,0:T(8,128)S(1)}, f32[256,2048]{1,0:T(8,128)}, u32[]{:S(2)}) copy-start(f32[256,2048]{1,0:T(8,128)} %copy-done.7) | copy-start | bytes 6291460
  347.3 292.6 %all-gather.25.cloned.1.call-start = ((), (), s32[]{:S(2)}) async-start(), calls=%async_computation.21 | async-start | bytes 9437184 | tf_op jit(solution)/shard_map/all_gather | solution.py:144
  348.0 310.7 %all-gather.31.cloned.1.call-start = ((), (), s32[]{:S(2)}) async-start(), calls=%async_computation.26 | async-start | bytes 5242880 | tf_op jit(solution)/shard_map/all_gather | solution.py:193
  457.4 83.4 %copy-start.93 = (bf16[2048]{0:T(1024)(128)(2,1)S(1)}, bf16[2048]{0:T(1024)(128)(2,1)}, u32[]{:S(2)}) copy-start(bf16[2048]{0:T(1024)(128)(2,1)} %param.40) | copy-start | bytes 12292
  457.4 257.7 %all-gather.27.cloned.1.call-start = ((), (), s32[]{:S(2)}) async-start(), calls=%async_computation.22 | async-start | bytes 9437184 | tf_op jit(solution)/shard_map/all_gather | solution.py:145
  458.2 339.3 %all-gather.23.cloned.1.call-start = ((), (), s32[]{:S(2)}) async-start(), calls=%async_computation.20 | async-start | bytes 5242880 | tf_op jit(solution)/shard_map/all_gather | solution.py:193
  458.4 25.9 %collective-permute-start.3 = (bf16[256,2048]{1,0:T(8,128)(2,1)S(1)}, bf16[256,2048]{1,0:T(8,128)(2,1)S(1)}, u32[]{:S(2)}, u32[]{:S(2)}) collective-permute-start(bf16[256,2048]{1,0:T(8,128)(2,1)S(1)} %get-tuple-element.483), channel_id=1, source_target_pairs={{0,1},{1,2},{2,3},{3,0},{4,5},{5,6},{6,7},{7,4},{8,9},{9,10},{10,1... | collective-permute-start | bytes 3145736 | tf_op jit(solution)/shard_map/ppermute | solution.py:215
  459.7 47.1 %collective-permute-start = (bf16[256,2048]{1,0:T(8,128)(2,1)S(1)}, bf16[256,2048]{1,0:T(8,128)(2,1)S(1)}, u32[]{:S(2)}, u32[]{:S(2)}) collective-permute-start(bf16[256,2048]{1,0:T(8,128)(2,1)S(1)} %get-tuple-element.482), channel_id=1, source_target_pairs={{0,1},{1,2},{2,3},{3,0},{4,5},{5,6},{6,7},{7,4},{8,9},{9,10},{10,1... | collective-permute-start | bytes 3145736 | tf_op jit(solution)/shard_map/ppermute | solution.py:215
  484.3 50.7 %collective-permute-start.4 = (bf16[256,2048]{1,0:T(8,128)(2,1)S(1)}, bf16[256,2048]{1,0:T(8,128)(2,1)}, u32[]{:S(2)}, u32[]{:S(2)}) collective-permute-start(bf16[256,2048]{1,0:T(8,128)(2,1)S(1)} %collective-permute-done.3), channel_id=1, source_target_pairs={{0,1},{1,2},{2,3},{3,0},{4,5},{5,6},{6,7},{7,4},{8,9},{9,10},{10,1... | collective-permute-start | bytes 3145736 | tf_op jit(solution)/shard_map/ppermute | solution.py:215
  506.7 73.2 %collective-permute-start.1 = (bf16[256,2048]{1,0:T(8,128)(2,1)S(1)}, bf16[256,2048]{1,0:T(8,128)(2,1)}, u32[]{:S(2)}, u32[]{:S(2)}) collective-permute-start(bf16[256,2048]{1,0:T(8,128)(2,1)S(1)} %collective-permute-done), channel_id=1, source_target_pairs={{0,1},{1,2},{2,3},{3,0},{4,5},{5,6},{6,7},{7,4},{8,9},{9,10},{10,1... | collective-permute-start | bytes 3145736 | tf_op jit(solution)/shard_map/ppermute | solution.py:215
  535.0 89.9 %collective-permute-start.5 = (bf16[256,2048]{1,0:T(8,128)(2,1)}, bf16[256,2048]{1,0:T(8,128)(2,1)}, u32[]{:S(2)}, u32[]{:S(2)}) collective-permute-start(bf16[256,2048]{1,0:T(8,128)(2,1)} %collective-permute-done.4), channel_id=1, source_target_pairs={{0,1},{1,2},{2,3},{3,0},{4,5},{5,6},{6,7},{7,4},{8,9},{9,10},{10,1... | collective-permute-start | bytes 3145736 | tf_op jit(solution)/shard_map/ppermute | solution.py:215
  579.9 166.6 %collective-permute-start.2 = (bf16[256,2048]{1,0:T(8,128)(2,1)}, bf16[256,2048]{1,0:T(8,128)(2,1)}, u32[]{:S(2)}, u32[]{:S(2)}) collective-permute-start(bf16[256,2048]{1,0:T(8,128)(2,1)} %collective-permute-done.1), channel_id=1, source_target_pairs={{0,1},{1,2},{2,3},{3,0},{4,5},{5,6},{6,7},{7,4},{8,9},{9,10},{10,1... | collective-permute-start | bytes 3145736 | tf_op jit(solution)/shard_map/ppermute | solution.py:215
  639.8 236.1 %reduce-scatter.27.cloned.1.call-start = ((), (), s32[]{:S(2)}) async-start(), calls=%async_computation.31 | async-start | bytes 5242880 | tf_op jit(solution)/shard_map/reduce_scatter | solution.py:230
  746.4 208.3 %reduce-scatter.23.cloned.1.call-start = ((), (), s32[]{:S(2)}) async-start(), calls=%async_computation.28 | async-start | bytes 5242880 | tf_op jit(solution)/shard_map/reduce_scatter | solution.py:230
  842.8 191.3 %reduce-scatter.21.cloned.1.call-start = ((), (), s32[]{:S(2)}) async-start(), calls=%async_computation.27 | async-start | bytes 5242880 | tf_op jit(solution)/shard_map/reduce_scatter | solution.py:205
  859.2 254.5 %reduce-scatter.17.cloned.1.call-start = ((), (), s32[]{:S(2)}) async-start(), calls=%async_computation.23 | async-start | bytes 5242880 | tf_op jit(solution)/shard_map/reduce_scatter | solution.py:205
  875.3 79.4 %copy-start.17 = (f32[256,2048]{1,0:T(8,128)S(1)}, f32[256,2048]{1,0:T(8,128)}, u32[]{:S(2)}) copy-start(f32[256,2048]{1,0:T(8,128)} %copy-done.16) | copy-start | bytes 6291460
  875.3 79.4 %copy-start.63 = (f32[2048]{0:T(1024)S(1)}, f32[2048]{0:T(1024)}, u32[]{:S(2)}) copy-start(f32[2048]{0:T(1024)} %param.45) | copy-start | bytes 24580
  875.3 79.4 %copy-start.75 = (f32[256]{0:T(256)S(1)}, f32[256]{0:T(256)}, u32[]{:S(2)}) copy-start(f32[256]{0:T(256)} %copy-done.74) | copy-start | bytes 3076
  875.4 328.8 %all-gather.33.cloned.1.call-start = ((), (), s32[]{:S(2)}) async-start(), calls=%async_computation.29 | async-start | bytes 5242880 | tf_op jit(solution)/shard_map/all_gather | solution.py:234
  1122.8 162.2 %all-gather.35.cloned.1.call-start = ((), (), s32[]{:S(2)}) async-start(), calls=%async_computation.32 | async-start | bytes 5242880 | tf_op jit(solution)/shard_map/all_gather | solution.py:234
  1124.0 429.9 %reduce-scatter.41.cloned.1.call-start = ((), (), s32[]{:S(2)}) async-start(), calls=%async_computation.40 | async-start | bytes 9437184 | tf_op jit(solution)/shard_map/reduce_scatter | solution.py:330
  1163.0 393.7 %reduce-scatter.39.cloned.1.call-start = ((), (), s32[]{:S(2)}) async-start(), calls=%async_computation.39 | async-start | bytes 9437184 | tf_op jit(solution)/shard_map/reduce_scatter | solution.py:327
  1193.9 391.2 %reduce-scatter.37.cloned.1.call-start = ((), (), s32[]{:S(2)}) async-start(), calls=%async_computation.38 | async-start | bytes 2359296 | tf_op jit(solution)/shard_map/reduce_scatter | solution.py:324
  1389.4 197.4 %reduce-scatter.35.cloned.1.call-start = ((), (), s32[]{:S(2)}) async-start(), calls=%async_computation.37 | async-start | bytes 2359296 | tf_op jit(solution)/shard_map/reduce_scatter | solution.py:321
  1501.8 86.8 %reduce-scatter.31.cloned.1.call-start = ((), (), s32[]{:S(2)}) async-start(), calls=%async_computation.35 | async-start | bytes 2359296 | tf_op jit(solution)/shard_map/reduce_scatter | solution.py:315
  1512.9 118.8 %reduce-scatter.33.cloned.1.call-start = ((), (), s32[]{:S(2)}) async-start(), calls=%async_computation.36 | async-start | bytes 2359296 | tf_op jit(solution)/shard_map/reduce_scatter | solution.py:318
  1523.6 187.3 %reduce-scatter.25.cloned.1.call-start = ((), (), s32[]{:S(2)}) async-start(), calls=%async_computation.30 | async-start | bytes 5242880 | tf_op jit(solution)/shard_map/reduce_scatter | solution.py:286
  1535.9 255.1 %reduce-scatter.29.cloned.1.call-start = ((), (), s32[]{:S(2)}) async-start(), calls=%async_computation.33 | async-start | bytes 5242880 | tf_op jit(solution)/shard_map/reduce_scatter | solution.py:286
  1548.8 380.0 %all-reduce.4.cloned.1.call-start = ((), (), s32[]{:S(2)}) async-start(), calls=%async_computation.34 | async-start | bytes 917504 | tf_op jit(solution)/shard_map/psum | solution.py:335
  1556.7 154.2 %copy-start.9 = (f32[256,2048]{1,0:T(8,128)S(1)}, f32[256,2048]{1,0:T(8,128)}, u32[]{:S(2)}) copy-start(f32[256,2048]{1,0:T(8,128)} %copy-done.7) | copy-start | bytes 6291460
  1556.7 154.2 %copy-start.61 = (f32[2048]{0:T(1024)S(1)}, f32[2048]{0:T(1024)}, u32[]{:S(2)}) copy-start(f32[2048]{0:T(1024)} %param.43) | copy-start | bytes 24580
  1556.7 154.2 %copy-start.71 = (f32[256]{0:T(256)S(1)}, f32[256]{0:T(256)}, u32[]{:S(2)}) copy-start(f32[256]{0:T(256)} %copy-done.70) | copy-start | bytes 3076
  1556.7 154.2 %copy-start.79 = (f32[256]{0:T(256)S(1)}, f32[256]{0:T(256)}, u32[]{:S(2)}) copy-start(f32[256]{0:T(256)} %copy-done.78) | copy-start | bytes 3076
  1559.8 231.2 %copy-start.73 = (f32[256]{0:T(256)S(1)}, f32[256]{0:T(256)}, u32[]{:S(2)}) copy-start(f32[256]{0:T(256)} %copy-done.72) | copy-start | bytes 3076
  1559.8 231.2 %copy-start.81 = (f32[256]{0:T(256)S(1)}, f32[256]{0:T(256)}, u32[]{:S(2)}) copy-start(f32[256]{0:T(256)} %copy-done.80) | copy-start | bytes 3076
  1713.1 83.0 %copy-start.87 = (s32[256]{0:T(256)S(1)}, s32[256]{0:T(256)}, u32[]{:S(2)}) copy-start(s32[256]{0:T(256)} %copy-done.86) | copy-start | bytes 3076
  1842.8 87.7 %copy-start.1 = (f32[50,2048]{1,0:T(8,128)S(1)}, f32[50,2048]{1,0:T(8,128)}, u32[]{:S(2)}) copy-start(f32[50,2048]{1,0:T(8,128)} %param.31) | copy-start | bytes 1228804
  (115 other events, 1137.7 us)
Sparse Core Ops, SparseCore 0:
  9.9 30.3 all-gather.16
  42.5 80.3 all-gather.12
  124.8 26.8 all-gather.18
  153.4 27.8 all-gather.14
  183.1 28.1 all-gather.20
  213.3 80.3 all-gather.28
  296.6 75.2 reduce-scatter.14
  374.3 77.2 reduce-scatter.18
  453.5 55.2 all-gather.24
  510.8 147.8 all-gather.30
  660.6 54.4 all-gather.26
  717.1 80.3 all-gather.22
  799.8 75.2 reduce-scatter.26
  877.4 77.2 reduce-scatter.22
  956.8 77.2 reduce-scatter.20
  1036.4 77.2 reduce-scatter.16
  1122.9 81.2 all-gather.32
  1205.6 79.2 all-gather.34
  1288.4 69.7 reduce-scatter.40
  1361.9 71.2 reduce-scatter.38
  1436.5 41.2 reduce-scatter.36
  1502.0 40.2 reduce-scatter.34
  1545.6 41.3 reduce-scatter.30
  1590.4 41.2 reduce-scatter.32
  1634.0 76.7 reduce-scatter.24
  1713.7 77.2 reduce-scatter.28
  1801.2 127.5 all-reduce.3
